TPU v7x, 32 devices: a whole 2x2x4 slice. The times are simulated.
32 devices in a mesh: pts: 8 (over y, x, core), out: 4 (over z).
Axes of the slice: x: 2, y: 2, z: 4, core: 2. Of those that a mesh axis runs over, the one named last changes fastest.
Arguments:
- points: bfloat16 [32768, 1024], P('pts'), may hold values from -6 to 6
- coefficients: float32 [32768, 1024], P('pts', 'out'), may hold values from -4 to 4
- residual: float32 [32768, 1024], P('pts', 'out'), may hold values from -6 to 6
- blocks: int32 [3, 512], replicated, may hold values from 0 to 32767, as said below
Outputs:
- coefficients_out: float32 [32768, 1024], P('pts', 'out')
- residual_out: float32 [32768, 1024], P('pts', 'out')
Inputs may be any that keep to these rules, and one draw needn't show every extreme that they name: `blocks`: the 512 indices of a step are distinct.
All inputs are finite; a program needn't handle non-finite values.
Results may differ from a plain program's by a relative error of at most 0.0003.
Values may be sent and summed in bfloat16 or wider, within the bound.
No kernel may reach another device: no remote copies, remote signals or barrier semaphores. Data moves between devices by JAX's collectives and lax.ppermute only.
A program may use at most 128 MiB of HBM per device.

v0:
```python
import jax
import jax.numpy as jnp
from jax import lax
from jax.sharding import PartitionSpec as P

RIDGE = 0.5


def kernel(left_rows, right_rows, inverse_width):
    left_sq = jnp.sum(jnp.square(left_rows.astype(jnp.float32)), axis=1)
    right_sq = jnp.sum(jnp.square(right_rows.astype(jnp.float32)), axis=1)
    inner = lax.dot_general(
        left_rows, right_rows, (((1,), (1,)), ((), ())), preferred_element_type=jnp.float32
    )
    return jnp.exp(-inverse_width * (left_sq[:, None] + right_sq[None, :] - 2.0 * inner))


def local(points, coefficients, residual, blocks):
    local_count = points.shape[0]
    inverse_width = 1.0 / points.shape[1]
    position = lax.axis_index("pts")
    for number in range(blocks.shape[0]):
        chosen = blocks[number]
        offsets = chosen - position * local_count
        is_owned = (offsets >= 0) & (offsets < local_count)
        clipped = jnp.clip(offsets, 0, local_count - 1)
        owned_rows = jnp.where(is_owned[:, None], points[clipped].astype(jnp.float32), 0.0)
        owned_res = jnp.where(is_owned[:, None], residual[clipped], 0.0)
        summed = lax.psum(owned_rows.astype(jnp.bfloat16), "pts")
        block_res = lax.psum(owned_res, "pts")
        kernel_rows = kernel(points, summed, inverse_width)
        block_kernel = kernel(summed, summed, inverse_width)
        block_size = chosen.shape[0]
        factor = jnp.linalg.cholesky(block_kernel + RIDGE * jnp.eye(block_size, dtype=jnp.float32))
        update = jax.scipy.linalg.cho_solve((factor, True), block_res)
        product = jnp.dot(kernel_rows, update, precision=lax.Precision.HIGHEST)
        own_update = jnp.where(is_owned[:, None], update, 0.0)
        coefficients = coefficients.at[clipped].add(own_update)
        placed = jnp.zeros_like(residual).at[clipped].add(own_update)
        residual = residual - product - RIDGE * placed
    return (coefficients, residual)


def solution(mesh):
    return jax.shard_map(
        local,
        mesh=mesh,
        in_specs=(P("pts", None), P("pts", "out"), P("pts", "out"), P()),
        out_specs=(P("pts", "out"), P("pts", "out")),
        check_vma=False,
    )
```

profile of v0, /device:TPU:0, one launch (start us, length us, event | category | flops | bytes accessed | tf_op | source)
XLA Modules:
  0.0 701.5 jit_solution(9983994958240367674)
XLA Ops:
  46.6 62.1 %all-reduce.13.cloned.1.call-done = (bf16[512,1024]{1,0:T(8,128)(2,1)}, bf16[512,1024]{1,0:T(8,128)(2,1)}, bf16[512,1024]{1,0:T(8,128)(2,1)}) async-done(((bf16[512,1024]{1,0:T(8,128)(2,1)}, bf16[512,1024]{1,0:T(8,128)(2,1)}, bf16[512,1024]{1,0:T(8,128)(2,1)}), (bf16[512,1024]{1,0:T(8,128)(2,1)}, bf16[512,1024]{1,0:T(8,128)(2,1)}, bf16[512,1024]{1,0:T(8,128)(2,1)})) %all-reduce.13.cloned.1.call-update) | async-done | bytes 3145744 | tf_op jit(solution)/shard_map/psum | solution.py:29
  113.3 11.7 %cholesky.518 = f32[128,128]{1,0:T(8,128)S(1)} custom-call(f32[128,128]{1,0:T(8,128)S(1)} %cholesky.612), custom_call_target="Cholesky" | custom-call | tf_op jit(solution)/shard_map/jit(cholesky)/cholesky | solution.py:34
  125.0 9.8 %custom-call.41 = f32[1,128,128]{1,2,0:T(8,128)S(1)} custom-call(f32[1,128,128]{2,1,0:T(8,128)S(1)} %get-tuple-element.72), custom_call_target="InvertDiagBlocksLowerTriangular" | custom-call | tf_op jit(solution)/shard_map/jit(cholesky)/cholesky | solution.py:34
  135.7 12.1 %cholesky.537 = f32[128,128]{1,0:T(8,128)S(1)} custom-call(f32[128,128]{1,0:T(8,128)S(1)} %cholesky.616), custom_call_target="Cholesky" | custom-call | tf_op jit(solution)/shard_map/jit(cholesky)/cholesky | solution.py:34
  149.2 9.8 %custom-call.42 = f32[1,128,128]{1,2,0:T(8,128)S(1)} custom-call(f32[1,128,128]{2,1,0:T(8,128)S(1)} %get-tuple-element.69), custom_call_target="InvertDiagBlocksLowerTriangular" | custom-call | tf_op jit(solution)/shard_map/jit(cholesky)/cholesky | solution.py:34
  159.7 11.7 %cholesky.558 = f32[128,128]{1,0:T(8,128)S(1)} custom-call(f32[128,128]{1,0:T(8,128)S(1)} %cholesky.621), custom_call_target="Cholesky" | custom-call | tf_op jit(solution)/shard_map/jit(cholesky)/cholesky | solution.py:34
  172.0 9.8 %custom-call.43 = f32[1,128,128]{1,2,0:T(8,128)S(1)} custom-call(f32[1,128,128]{2,1,0:T(8,128)S(1)} %get-tuple-element.66), custom_call_target="InvertDiagBlocksLowerTriangular" | custom-call | tf_op jit(solution)/shard_map/jit(cholesky)/cholesky | solution.py:34
  182.4 11.9 %cholesky.575 = f32[128,128]{1,0:T(8,128)S(1)} custom-call(f32[128,128]{1,0:T(8,128)S(1)} %convolution_subtract_fusion.24), custom_call_target="Cholesky" | custom-call | tf_op jit(solution)/shard_map/jit(cholesky)/cholesky | solution.py:34
  212.4 11.7 %cholesky.446 = f32[128,128]{1,0:T(8,128)S(1)} custom-call(f32[128,128]{1,0:T(8,128)S(1)} %cholesky.599), custom_call_target="Cholesky" | custom-call | tf_op jit(solution)/shard_map/jit(cholesky)/cholesky | solution.py:34
  224.2 9.8 %custom-call.37 = f32[1,128,128]{1,2,0:T(8,128)S(1)} custom-call(f32[1,128,128]{2,1,0:T(8,128)S(1)} %get-tuple-element.82), custom_call_target="InvertDiagBlocksLowerTriangular" | custom-call | tf_op jit(solution)/shard_map/jit(cholesky)/cholesky | solution.py:34
  236.6 11.7 %cholesky.465 = f32[128,128]{1,0:T(8,128)S(1)} custom-call(f32[128,128]{1,0:T(8,128)S(1)} %cholesky.603), custom_call_target="Cholesky" | custom-call | tf_op jit(solution)/shard_map/jit(cholesky)/cholesky | solution.py:34
  249.7 10.2 %custom-call.38 = f32[1,128,128]{1,2,0:T(8,128)S(1)} custom-call(f32[1,128,128]{2,1,0:T(8,128)S(1)} %get-tuple-element.79), custom_call_target="InvertDiagBlocksLowerTriangular" | custom-call | tf_op jit(solution)/shard_map/jit(cholesky)/cholesky | solution.py:34
  261.5 11.7 %cholesky.486 = f32[128,128]{1,0:T(8,128)S(1)} custom-call(f32[128,128]{1,0:T(8,128)S(1)} %cholesky.608), custom_call_target="Cholesky" | custom-call | tf_op jit(solution)/shard_map/jit(cholesky)/cholesky | solution.py:34
  273.9 9.8 %custom-call.39 = f32[1,128,128]{1,2,0:T(8,128)S(1)} custom-call(f32[1,128,128]{2,1,0:T(8,128)S(1)} %get-tuple-element.76), custom_call_target="InvertDiagBlocksLowerTriangular" | custom-call | tf_op jit(solution)/shard_map/jit(cholesky)/cholesky | solution.py:34
  285.2 11.9 %cholesky.503 = f32[128,128]{1,0:T(8,128)S(1)} custom-call(f32[128,128]{1,0:T(8,128)S(1)} %convolution_subtract_fusion.25), custom_call_target="Cholesky" | custom-call | tf_op jit(solution)/shard_map/jit(cholesky)/cholesky | solution.py:34
  316.5 11.7 %cholesky.374 = f32[128,128]{1,0:T(8,128)S(1)} custom-call(f32[128,128]{1,0:T(8,128)S(1)} %cholesky.586), custom_call_target="Cholesky" | custom-call | tf_op jit(solution)/shard_map/jit(cholesky)/cholesky | solution.py:34
  328.2 9.8 %custom-call.33 = f32[1,128,128]{1,2,0:T(8,128)S(1)} custom-call(f32[1,128,128]{2,1,0:T(8,128)S(1)} %get-tuple-element.92), custom_call_target="InvertDiagBlocksLowerTriangular" | custom-call | tf_op jit(solution)/shard_map/jit(cholesky)/cholesky | solution.py:34
  340.7 11.7 %cholesky.393 = f32[128,128]{1,0:T(8,128)S(1)} custom-call(f32[128,128]{1,0:T(8,128)S(1)} %cholesky.590), custom_call_target="Cholesky" | custom-call | tf_op jit(solution)/shard_map/jit(cholesky)/cholesky | solution.py:34
  353.8 10.2 %custom-call.34 = f32[1,128,128]{1,2,0:T(8,128)S(1)} custom-call(f32[1,128,128]{2,1,0:T(8,128)S(1)} %get-tuple-element.89), custom_call_target="InvertDiagBlocksLowerTriangular" | custom-call | tf_op jit(solution)/shard_map/jit(cholesky)/cholesky | solution.py:34
  365.6 11.7 %cholesky.414 = f32[128,128]{1,0:T(8,128)S(1)} custom-call(f32[128,128]{1,0:T(8,128)S(1)} %cholesky.595), custom_call_target="Cholesky" | custom-call | tf_op jit(solution)/shard_map/jit(cholesky)/cholesky | solution.py:34
  378.0 9.8 %custom-call.35 = f32[1,128,128]{1,2,0:T(8,128)S(1)} custom-call(f32[1,128,128]{2,1,0:T(8,128)S(1)} %get-tuple-element.86), custom_call_target="InvertDiagBlocksLowerTriangular" | custom-call | tf_op jit(solution)/shard_map/jit(cholesky)/cholesky | solution.py:34
  389.3 11.9 %cholesky.431 = f32[128,128]{1,0:T(8,128)S(1)} custom-call(f32[128,128]{1,0:T(8,128)S(1)} %convolution_subtract_fusion.26), custom_call_target="Cholesky" | custom-call | tf_op jit(solution)/shard_map/jit(cholesky)/cholesky | solution.py:34
  405.5 11.9 %while.6 = (s32[]{:T(128)}, f32[512,512]{1,0:T(8,128)}, s32[4,2]{0,1:T(2,128)S(1)}, f32[4,128,128]{2,1,0:T(8,128)S(1)}, s32[]{:T(128)}) while((s32[]{:T(128)}, f32[512,512]{1,0:T(8,128)}, s32[4,2]{0,1:T(2,128)S(1)}, f32[4,128,128]{2,1,0:T(8,128)S(1)}, s32[]{:T(128)}) %tuple.99), condition=%wide.while_cond, body=%wide.while_body.sunk | while | flops 2 | bytes 131181 | solution.py:35
  417.4 11.5 %fusion.237 = f32[512,4096]{0,1:T(8,128)} fusion(bf16[512,1024]{1,0:T(8,128)(2,1)} %get-tuple-element.54, bf16[4096,1024]{1,0:T(8,128)(2,1)} %param.7), kind=kOutput, calls=%fused_computation.375 | convolution fusion | flops 4294967296 | bytes 17825792 | tf_op jit(solution)/shard_map/dot_general | solution.py:12
  428.9 39.3 %custom-call.36 = f32[4,128,128]{1,2,0:T(8,128)S(1)} custom-call(f32[4,128,128]{2,1,0:T(8,128)S(1)} %get-tuple-element.24), custom_call_target="InvertDiagBlocksLowerTriangular" | custom-call | tf_op jit(solution)/shard_map/jit(_cho_solve)/triangular_solve | solution.py:35
  485.5 12.8 %fusion.21 = f32[4096,256]{1,0:T(8,128)} fusion(f32[4096,256]{1,0:T(8,128)} %param.9, f32[512,4096]{0,1:T(8,128)} %fusion.237, f32[4096,256]{1,0:T(8,128)} %scatter_custom_fusion.1, f32[512]{0:T(512)S(1)} %multiply_reduce_fusion.3, f32[4096]{0:T(1024)S(1)} %multiply_reduce_fusion, f32[128,256]{1,0:T(8,128)S(1)} %fusion.197, f32[128,256]{1,0:T(8,128)S(1)} %fusion.195, ...), kind=kOutput, calls=%fused_computation.38 | convolution fusion | flops 6454378496 | bytes 21514240 | tf_op jit(solution)/shard_map/dot_general | solution.py:36
  504.7 11.5 %fusion.238 = f32[512,4096]{0,1:T(8,128)} fusion(bf16[512,1024]{1,0:T(8,128)(2,1)} %get-tuple-element.55, bf16[4096,1024]{1,0:T(8,128)(2,1)} %param.7), kind=kOutput, calls=%fused_computation.376 | convolution fusion | flops 4294967296 | bytes 17825792 | tf_op jit(solution)/shard_map/dot_general | solution.py:12
  516.3 40.5 %custom-call.40 = f32[4,128,128]{1,2,0:T(8,128)S(1)} custom-call(f32[4,128,128]{2,1,0:T(8,128)} %copy-done.3), custom_call_target="InvertDiagBlocksLowerTriangular" | custom-call | tf_op jit(solution)/shard_map/jit(_cho_solve)/triangular_solve | solution.py:35
  574.1 12.9 %fusion.27 = f32[4096,256]{1,0:T(8,128)} fusion(f32[4096,256]{1,0:T(8,128)} %fusion.21, f32[512,4096]{0,1:T(8,128)} %fusion.238, f32[4096,256]{1,0:T(8,128)} %scatter_custom_fusion.3, f32[512]{0:T(512)S(1)} %multiply_reduce_fusion.2, f32[4096]{0:T(1024)S(1)} %multiply_reduce_fusion, f32[128,256]{1,0:T(8,128)S(1)} %fusion.204, f32[128,256]{1,0:T(8,128)S(1)} %fusion.202, ...), kind=kOutput, calls=%fused_computation.40 | convolution fusion | flops 6454378496 | bytes 21514240 | tf_op jit(solution)/shard_map/dot_general | solution.py:36
  591.8 11.5 %fusion.239 = f32[512,4096]{0,1:T(8,128)} fusion(bf16[512,1024]{1,0:T(8,128)(2,1)} %get-tuple-element.56, bf16[4096,1024]{1,0:T(8,128)(2,1)} %param.7), kind=kOutput, calls=%fused_computation.377 | convolution fusion | flops 4294967296 | bytes 17825792 | tf_op jit(solution)/shard_map/dot_general | solution.py:12
  603.3 40.1 %custom-call.44 = f32[4,128,128]{1,2,0:T(8,128)S(1)} custom-call(f32[4,128,128]{2,1,0:T(8,128)} %copy-done.2), custom_call_target="InvertDiagBlocksLowerTriangular" | custom-call | tf_op jit(solution)/shard_map/jit(_cho_solve)/triangular_solve | solution.py:35
  673.6 13.0 %fusion.33 = f32[4096,256]{1,0:T(8,128)} fusion(f32[4096,256]{1,0:T(8,128)} %fusion.27, f32[512,4096]{0,1:T(8,128)} %fusion.239, f32[4096,256]{1,0:T(8,128)} %scatter_custom_fusion.5, f32[512]{0:T(512)S(1)} %multiply_reduce_fusion.1, f32[4096]{0:T(1024)S(1)} %multiply_reduce_fusion, f32[128,256]{1,0:T(8,128)S(1)} %fusion.211, f32[128,256]{1,0:T(8,128)S(1)} %fusion.209, ...), kind=kOutput, calls=%fused_computation.42 | convolution fusion | flops 6454378496 | bytes 21514240 | tf_op jit(solution)/shard_map/dot_general | solution.py:36
  (199 shorter events, 209.4 us)
Async XLA Ops:
  7.2 4.5 copy-start.4
  7.2 101.5 %all-reduce.13.cloned.1.call-start = ((), (), s32[]{:S(2)}) async-start(), calls=%async_computation.3 | async-start | bytes 6291456 | tf_op jit(solution)/shard_map/psum | solution.py:29
  36.4 431.9 %all-reduce.7.cloned.1.call-start = ((), (), s32[]{:S(2)}) async-start(), calls=%async_computation | async-start | bytes 1048576 | tf_op jit(solution)/shard_map/psum | solution.py:30
  41.1 518.8 %all-reduce.9.cloned.1.call-start = ((), (), s32[]{:S(2)}) async-start(), calls=%async_computation.1 | async-start | bytes 1048576 | tf_op jit(solution)/shard_map/psum | solution.py:30
  206.1 0.7 copy-start.2
  211.4 1.0 copy-start
  308.8 6.7 copy-start.3
  315.5 1.0 copy-start.1
  504.7 154.8 %all-reduce.11.cloned.1.call-start = ((), (), s32[]{:S(2)}) async-start(), calls=%async_computation.2 | async-start | bytes 1048576 | tf_op jit(solution)/shard_map/psum | solution.py:30
Sparse Core Ops, SparseCore 0:
  36.5 72.1 all-reduce.12
  111.8 55.1 all-reduce.6
  504.8 55.0 all-reduce.8
  591.9 54.4 all-reduce.10
where the time goes:
time: 710 us; the launch traced here: 702 us
  other arithmetic  421 us (59%)
  matrix products  120 us (17%)
  local copies, waits for them, and re-layouts  71.3 us (10%)
  waiting for transfers between devices  65.4 us (9%)
  between operations  22.8 us (3%)
    another operation x45, other arithmetic, local(): jnp.linalg.cholesky(block_kernel + RIDGE * jnp.eye(block_size, dtype=jnp....  239 us
    another operation x7, other arithmetic, local(): update = jax.scipy.linalg.cho_solve((factor, True), block_res)  121 us
    psum x1, waiting for transfers between devices, local(): summed = lax.psum(owned_rows.astype(jnp.bfloat16), 'pts')  62.1 us
    dot_general x6, matrix products, kernel(): lax.dot_general(left_rows, right_rows, (((1,), (1,)), ((), ())), preferre...  42 us
    dot_general x3, matrix products, local(): product = jnp.dot(kernel_rows, update, precision=lax.Precision.HIGHEST)  38.7 us
    another operation x40, local copies, waits for them, and re-layouts, local(): update = jax.scipy.linalg.cho_solve((factor, True), block_res)  28.3 us
    another operation x42, matrix products, local(): update = jax.scipy.linalg.cho_solve((factor, True), block_res)  26.9 us
    scatter-add x3, other arithmetic, local(): coefficients = coefficients.at[clipped].add(own_update)  24 us
  transfers between devices with their start and end apart: 4, of which 2 were waited for; matrix products, arithmetic and copies ran while one was open for 68% of the time, Pallas kernels for 0%

commit v1 on v0

v1 whole, which is shorter than its diff:
```python
import functools

import jax
import jax.numpy as jnp
from jax import lax
from jax.experimental import pallas as pl
from jax.experimental.pallas import tpu as pltpu
from jax.sharding import PartitionSpec as P

RIDGE = 0.5
PANEL = 128
GROUP = 4
HIGHEST = lax.Precision.HIGHEST
NT = (((1,), (1,)), ((), ()))
TN = (((0,), (0,)), ((), ()))


def dot32(a, b, dims=(((1,), (0,)), ((), ()))):
    return lax.dot_general(a, b, dims, precision=HIGHEST, preferred_element_type=jnp.float32)


def spread_lane(tile, lane):
    return jnp.broadcast_to(tile[:, lane : lane + 1], tile.shape)


def spread_row(tile, row):
    return jnp.broadcast_to(tile[row : row + 1, :], tile.shape)


def eliminate(tiles, start):
    lanes = lax.broadcasted_iota(jnp.int32, (8, PANEL), 1)
    subs = lax.broadcasted_iota(jnp.int32, (8, PANEL), 0)
    first, offset = start // 8, start % 8
    in_group = (lanes >= start) & (lanes < start + GROUP)
    head = tiles[first]
    columns = [[spread_lane(tiles[t], start + q) for t in range(first, len(tiles))] for q in range(GROUP)]
    rows = []
    for q in range(GROUP):
        own = jnp.where(lanes == start + q, 1.0, 0.0)
        rows.append(jnp.where(in_group, own, spread_row(head, offset + q)))
    pivot = {}
    for m in range(GROUP):
        for q in range(m, GROUP):
            pivot[q, m] = spread_row(columns[m][0], offset + q)
    roots, scaled = [], []
    for m in range(GROUP):
        root = lax.rsqrt(pivot[m, m])
        inverse = root * root
        roots.append(root)
        factor = {q: pivot[q, m] * inverse for q in range(m + 1, GROUP)}
        for q in range(m + 1, GROUP):
            for n in range(m + 1, q + 1):
                pivot[q, n] = pivot[q, n] - factor[q] * pivot[n, m]
        for q in range(m + 1, GROUP):
            rows[q] = rows[q] - factor[q] * rows[m]
            columns[q] = [c - factor[q] * b for c, b in zip(columns[q], columns[m])]
        scaled.append(rows[m] * inverse)
    out = list(tiles)
    for t in range(first, len(tiles)):
        if t == first and offset + GROUP == 8:
            continue
        value = jnp.where(in_group, 0.0, tiles[t])
        for m in range(GROUP):
            value = value - columns[m][t - first] * scaled[m]
        out[t] = value
    top = jnp.where(subs < offset, head, out[first])
    for m in range(GROUP):
        done = jnp.where(lanes < start + GROUP, rows[m] * roots[m], 0.0)
        top = jnp.where(subs == offset + m, done, top)
    out[first] = top
    return out


def factor_kernel(steps, size, scale, points_ref, col_ref, row_ref, inv_ref, cross_ref, norm_ref, work):
    def rows_of(s):
        return points_ref[s * size : (s + 1) * size, :]

    eye = lax.broadcasted_iota(jnp.int32, (size, size), 0) == lax.broadcasted_iota(jnp.int32, (size, size), 1)
    norm_cols = []
    for s in range(steps):
        inner = lax.dot_general(rows_of(s), rows_of(s), NT, preferred_element_type=jnp.float32)
        diagonal = jnp.where(eye, inner, 0.0)
        norm_col = jnp.sum(diagonal, axis=1, keepdims=True)
        norm_row = jnp.sum(diagonal, axis=0, keepdims=True)
        norm_cols.append(norm_col)
        norm_ref[:, s * size : (s + 1) * size] = norm_row
        work[s] = jnp.exp((2.0 * inner - norm_col - norm_row) * scale) + jnp.where(eye, RIDGE, 0.0)
    pair = 0
    for s in range(steps):
        for t in range(s):
            inner = lax.dot_general(rows_of(s), rows_of(t), NT, preferred_element_type=jnp.float32)
            norm_row = norm_ref[:, t * size : (t + 1) * size]
            same = col_ref[s * size : (s + 1) * size, :] == row_ref[:, t * size : (t + 1) * size]
            cross_ref[pair] = jnp.exp((2.0 * inner - norm_cols[s] - norm_row) * scale) + jnp.where(same, RIDGE, 0.0)
            pair += 1
    panels = size // PANEL
    for k in range(panels):
        low, high = k * PANEL, (k + 1) * PANEL
        blocks = []
        for s in range(steps):
            blocks.append([work[s, low + 8 * t : low + 8 * t + 8, low:high] for t in range(PANEL // 8)])
        for start in range(0, PANEL, GROUP):
            blocks = [eliminate(tiles, start) for tiles in blocks]
        for s in range(steps):
            inv_ref[s, low:high, low:high] = jnp.concatenate(blocks[s], axis=0)
        for s in range(steps):
            tri = inv_ref[s, low:high, low:high]
            if high < size:
                inv_ref[s, low:high, high:] = jnp.zeros((PANEL, size - high), jnp.float32)
                below = dot32(work[s, high:, low:high], tri, NT)
                work[s, high:, low:high] = below
                work[s, high:, high:] = work[s, high:, high:] - dot32(below, below, NT)
            if low > 0:
                left = dot32(work[s, low:high, :low], inv_ref[s, :low, :low])
                inv_ref[s, low:high, :low] = -dot32(tri, left)


def solve_kernel(steps, size, inv_ref, cross_ref, res_ref, up_ref, high_ref, low_ref, half_ref):
    pair = 0
    total = None
    for s in range(steps):
        here = slice(s * size, (s + 1) * size)
        rhs = res_ref[here, :]
        for t in range(s):
            rhs = rhs - dot32(cross_ref[pair], up_ref[t * size : (t + 1) * size, :])
            pair += 1
        update = dot32(inv_ref[s], dot32(inv_ref[s], rhs), TN)
        up_ref[here, :] = update
        high = update.astype(jnp.bfloat16)
        high_ref[here, :] = high
        low_ref[here, :] = (update - high.astype(jnp.float32)).astype(jnp.bfloat16)
        part = jnp.sum(update, axis=0, keepdims=True)
        total = part if total is None else total + part
    half_ref[...] = 0.5 * total


def apply_kernel(scale, tile, points_ref, chosen_ref, norm_ref, row_ref, high_ref, low_ref, half_ref, res_ref, out_ref):
    mine = points_ref[...]
    wide = mine.astype(jnp.float32)
    norm_col = jnp.sum(wide * wide, axis=1, keepdims=True)
    inner = lax.dot_general(mine, chosen_ref[...], NT, preferred_element_type=jnp.float32)
    ids = lax.broadcasted_iota(jnp.int32, (tile, 1), 0) + pl.program_id(0) * tile
    shifted = jnp.where(ids == row_ref[...], RIDGE - 0.5, -0.5)
    values = jnp.exp((2.0 * inner - norm_col - norm_ref[...]) * scale) + shifted
    high = values.astype(jnp.bfloat16)
    low = (values - high.astype(jnp.float32)).astype(jnp.bfloat16)
    product = jnp.dot(high, high_ref[...], preferred_element_type=jnp.float32)
    product += jnp.dot(high, low_ref[...], preferred_element_type=jnp.float32)
    product += jnp.dot(low, high_ref[...], preferred_element_type=jnp.float32)
    out_ref[...] = res_ref[...] - product - half_ref[...]


def local(points, coefficients, residual, blocks):
    local_count, features = points.shape
    outs = residual.shape[1]
    steps, size = blocks.shape
    scale = 1.0 / features
    position = lax.axis_index("pts")
    offsets = blocks.reshape(-1) - position * local_count
    is_owned = (offsets >= 0) & (offsets < local_count)
    clipped = jnp.clip(offsets, 0, local_count - 1)
    owned_rows = jnp.where(is_owned[:, None], points[clipped], jnp.bfloat16(0.0))
    owned_res = jnp.where(is_owned[:, None], residual[clipped], 0.0)
    chosen = lax.psum(owned_rows, "pts")
    block_res = lax.psum(owned_res, "pts")

    count = steps * size
    pairs = steps * (steps - 1) // 2
    f32 = jnp.float32
    params = pltpu.CompilerParams(vmem_limit_bytes=60 * 2**20)
    inverse, cross, norms = pl.pallas_call(
        functools.partial(factor_kernel, steps, size, scale),
        out_shape=(
            jax.ShapeDtypeStruct((steps, size, size), f32),
            jax.ShapeDtypeStruct((pairs, size, size), f32),
            jax.ShapeDtypeStruct((1, count), f32),
        ),
        scratch_shapes=[pltpu.VMEM((steps, size, size), f32)],
        compiler_params=params,
        name="factor",
    )(chosen, offsets[:, None], offsets[None, :])
    update, high, low, half = pl.pallas_call(
        functools.partial(solve_kernel, steps, size),
        out_shape=(
            jax.ShapeDtypeStruct((count, outs), f32),
            jax.ShapeDtypeStruct((count, outs), jnp.bfloat16),
            jax.ShapeDtypeStruct((count, outs), jnp.bfloat16),
            jax.ShapeDtypeStruct((1, outs), f32),
        ),
        compiler_params=params,
        name="solve",
    )(inverse, cross, block_res)
    tile = 512

    def whole(shape):
        return pl.BlockSpec(shape, lambda i: (0, 0), pipeline_mode=pl.Buffered(1))

    residual_out = pl.pallas_call(
        functools.partial(apply_kernel, scale, tile),
        grid=(local_count // tile,),
        in_specs=[
            pl.BlockSpec((tile, features), lambda i: (i, 0)),
            whole((count, features)),
            whole((1, count)),
            whole((1, count)),
            whole((count, outs)),
            whole((count, outs)),
            whole((1, outs)),
            pl.BlockSpec((tile, outs), lambda i: (i, 0)),
        ],
        out_specs=pl.BlockSpec((tile, outs), lambda i: (i, 0)),
        out_shape=jax.ShapeDtypeStruct((local_count, outs), f32),
        compiler_params=params,
        name="apply",
    )(points, chosen, norms, offsets[None, :], high, low, half, residual)
    own_update = jnp.where(is_owned[:, None], update, 0.0)
    coefficients = coefficients.at[clipped].add(own_update)
    return (coefficients, residual_out)


def solution(mesh):
    return jax.shard_map(
        local,
        mesh=mesh,
        in_specs=(P("pts", None), P("pts", "out"), P("pts", "out"), P()),
        out_specs=(P("pts", "out"), P("pts", "out")),
        check_vma=False,
    )
```

time: 710 us -> 248 us (0.35)
  other arithmetic: 421 us -> 19.2 us
  matrix products: 120 us -> 0 us
  Pallas kernels: 0 us -> 106 us
  local copies, waits for them, and re-layouts: 71.3 us -> 23.6 us
  waiting for transfers between devices: 65.4 us -> 80.8 us
  between operations: 22.8 us -> 14.3 us
    another operation x52 -> x0, other arithmetic: 360 us -> none  [the longest x45 239 us: local(): jnp.linalg.cholesky(block_kernel + RIDGE * jnp.eye(block_size, dtype=jnp....]
    pallas_call x0 -> x3, Pallas kernels: none -> 106 us  [the longest x1 44.3 us: local(): pl.pallas_call(functools.partial(factor_kernel, steps, size, scale), out_...]
    dot_general x9 -> x0, matrix products: 80.7 us -> none  [the longest x6 42 us: kernel(): lax.dot_general(left_rows, right_rows, (((1,), (1,)), ((), ())), preferre...]
    another operation x60 -> x0, matrix products: 39.8 us -> none  [the longest x42 26.9 us: local(): update = jax.scipy.linalg.cho_solve((factor, True), block_res)]
    another operation x52 -> x0, local copies, waits for them, and re-layouts: 28.8 us -> none  [the longest x40 28.3 us: local(): update = jax.scipy.linalg.cho_solve((factor, True), block_res)]
    scatter-add x3 -> x0, other arithmetic: 18.2 us -> none  [local(): placed = jnp.zeros_like(residual).at[clipped].add(own_update)]
    psum x3 -> x1, waiting for transfers between devices: 3.18 us -> 17.8 us  [local(): block_res = lax.psum(owned_res, 'pts')]
    gather x3 -> x1, local copies, waits for them, and re-layouts: 21.6 us -> 11.6 us  [local(): points[clipped]]
  transfers between devices with their start and end apart: 4 -> 2, of which waited for: 2 -> 2; matrix products, arithmetic and copies ran while one was open for 68% -> 4% of each run, Pallas kernels for 0% -> 18%
where the time goes in v1:
time: 248 us; the launch traced here: 244 us
  Pallas kernels  106 us (43%)
  waiting for transfers between devices  80.8 us (33%)
  local copies, waits for them, and re-layouts  23.6 us (10%)
  other arithmetic  19.2 us (8%)
  between operations  14.3 us (6%)
    psum x1, waiting for transfers between devices, local(): chosen = lax.psum(owned_rows, 'pts')  63 us
    pallas_call x1, Pallas kernels, local(): pl.pallas_call(functools.partial(factor_kernel, steps, size, scale), out_...  44.3 us
    pallas_call x1, Pallas kernels, local(): pl.pallas_call(functools.partial(apply_kernel, scale, tile), grid=(local_...  43.5 us
    pallas_call x1, Pallas kernels, local(): pl.pallas_call(functools.partial(solve_kernel, steps, size), out_shape=(j...  18.4 us
    psum x1, waiting for transfers between devices, local(): block_res = lax.psum(owned_res, 'pts')  17.8 us
    scatter-add x1, other arithmetic, local(): coefficients = coefficients.at[clipped].add(own_update)  15.5 us
    gather x1, local copies, waits for them, and re-layouts, local(): points[clipped]  11.6 us
    gather x1, local copies, waits for them, and re-layouts, local(): owned_res = jnp.where(is_owned[:, None], residual[clipped], 0.0)  6.38 us
  transfers between devices with their start and end apart: 2, of which 2 were waited for; matrix products, arithmetic and copies ran while one was open for 4% of the time, Pallas kernels for 18%

profile of v1, /device:TPU:0, one launch (start us, length us, event | category | flops | bytes accessed | tf_op | source)
XLA Modules:
  0.0 244.2 jit_solution(8050361715827880065)
XLA Ops:
  7.2 0.0 copy-start.1
  7.2 0.0 all-reduce.3.cloned.1.call-start
  7.2 4.5 %copy.13 = f32[4096,256]{1,0:T(8,128)} copy(f32[4096,256]{1,0:T(8,128)} %param.5) | data formatting | bytes 8388608
  11.7 0.0 copy-done.1
  11.7 0.0 copy-start
  11.8 11.6 %gather_fusion = bf16[1536,1024]{1,0:T(8,128)(2,1)S(1)} fusion(bf16[4096,1024]{1,0:T(8,128)(2,1)} %points_ref.1, s32[2048]{0:T(1024)S(1)} %pad_clamp_fusion), kind=kCustom, calls=%fused_computation | custom fusion | bytes 6297600 | tf_op jit(solution)/shard_map/gather | solution.py:162
  23.4 2.1 broadcast_select_fusion
  25.5 0.0 all-reduce.3.cloned.1.call-update
  25.5 0.0 all-reduce.5.cloned.1.call-start
  25.6 6.4 %gather_fusion.1 = f32[1536,256]{1,0:T(8,128)S(1)} fusion(f32[4096,256]{1,0:T(8,128)} %res_ref.1, s32[2048]{0:T(1024)S(1)} %pad_clamp_fusion), kind=kCustom, calls=%fused_computation.1 | custom fusion | bytes 3151872 | tf_op jit(solution)/shard_map/gather | solution.py:163
  31.9 1.5 broadcast_select_fusion.1
  33.4 0.0 all-reduce.5.cloned.1.call-update
  33.5 0.0 copy-done
  33.5 1.2 copy.6.col_ref
  34.7 63.0 %all-reduce.3.cloned.1.call-done.points_ref.chosen_ref = bf16[1536,1024]{1,0:T(8,128)(2,1)} async-done(((bf16[1536,1024]{1,0:T(8,128)(2,1)}), bf16[1536,1024]{1,0:T(8,128)(2,1)}) %all-reduce.3.cloned.1.call-update) | async-done | bytes 3145744 | tf_op jit(solution)/shard_map/psum | solution.py:164
  97.7 44.3 %factor.1 = (f32[3,512,512]{2,1,0:T(8,128)}, f32[3,512,512]{2,1,0:T(8,128)}, f32[1,1536]{1,0:T(1,128)}) custom-call(bf16[1536,1024]{1,0:T(8,128)(2,1)} %all-reduce.3.cloned.1.call-done.points_ref.chosen_ref, s32[1536,1]{1,0:T(8,128)} %copy.6.col_ref, s32[1,1536]{1,0:T(1,128)} %bitcast.10), custom_call_target="tpu_custom_call" | custom-call | tf_op jit(solution)/shard_map/factor/pallas_call | solution.py:171
  142.0 17.8 %all-reduce.5.cloned.1.call-done.res_ref = f32[1536,256]{1,0:T(8,128)} async-done(((f32[1536,256]{1,0:T(8,128)}), f32[1536,256]{1,0:T(8,128)}) %all-reduce.5.cloned.1.call-update) | async-done | bytes 1572880 | tf_op jit(solution)/shard_map/psum | solution.py:165
  159.8 18.4 %solve.1 = (f32[1536,256]{1,0:T(8,128)}, bf16[1536,256]{1,0:T(8,128)(2,1)}, bf16[1536,256]{1,0:T(8,128)(2,1)}, f32[1,256]{1,0:T(1,128)}) custom-call(f32[3,512,512]{2,1,0:T(8,128)} %get-tuple-element.9.inv_ref, f32[3,512,512]{2,1,0:T(8,128)} %get-tuple-element.10.cross_ref, f32[1536,256]{1,0:T(8,128)} %all-reduce.5.cloned.1.call-done.res_ref), custom_call_target="tpu_custom_call" | custom-call | tf_op jit(solution)/shard_map/solve/pallas_call | solution.py:182
  178.2 15.5 %scatter_custom_fusion = f32[4096,256]{1,0:T(8,128)} fusion(f32[4096,256]{1,0:T(8,128)} %copy.13, s32[1536]{0:T(1024)S(1)} %fusion.4, f32[1536,256]{1,0:T(8,128)} %get-tuple-element.11, f32[]{:T(128)} %constant.6.clone.1, pred[1536]{0:T(1024)(128)(4,1)S(1)} %and.12), kind=kCustom, calls=%fused_computation.4 | custom fusion | flops 786432 | bytes 5769728 | tf_op jit(solution)/shard_map/scatter-add | solution.py:217
  193.7 43.5 %apply.1 = f32[4096,256]{1,0:T(8,128)} custom-call(bf16[4096,1024]{1,0:T(8,128)(2,1)} %points_ref.1, bf16[1536,1024]{1,0:T(8,128)(2,1)} %all-reduce.3.cloned.1.call-done.points_ref.chosen_ref, f32[1,1536]{1,0:T(1,128)} %get-tuple-element.12.norm_ref, s32[1,1536]{1,0:T(1,128)} %bitcast.11, bf16[1536,256]{1,0:T(8,128)(2,1)} %get-tuple-element.13.high_ref, ...), custom_call_target="tpu_custom_call" | custom-call | tf_op jit(solution)/shard_map/apply/pallas_call | solution.py:198
  (6 shorter events, 0.1 us)
Async XLA Ops:
  7.2 4.5 %copy-start.1 = (s32[3,512]{1,0:T(4,128)S(1)}, s32[3,512]{1,0:T(4,128)}, u32[]{:S(2)}) copy-start(s32[3,512]{1,0:T(4,128)} %param.7) | copy-start | bytes 18436
  7.2 90.5 %all-reduce.3.cloned.1.call-start = ((), (), s32[]{:S(2)}) async-start(), calls=%async_computation | async-start | bytes 6291456 | tf_op jit(solution)/shard_map/psum | solution.py:164
  11.7 21.7 %copy-start = (s32[1,1,3,512]{3,1,2,0:T(1,128)}, s32[1,1,3,512]{3,1,2,0:T(1,128)S(1)}, u32[]{:S(2)}) copy-start(s32[1,1,3,512]{3,1,2,0:T(1,128)S(1)} %copy.7) | copy-start | bytes 18436
  25.5 134.3 %all-reduce.5.cloned.1.call-start = ((), (), s32[]{:S(2)}) async-start(), calls=%async_computation.1 | async-start | bytes 3145728 | tf_op jit(solution)/shard_map/psum | solution.py:165
Sparse Core Ops, SparseCore 0:
  25.6 72.0 all-reduce.2
  100.9 58.8 all-reduce.4
